TPU v7x, 32 devices: a whole 2x2x4 slice. The times are simulated.
32 devices in a mesh: fsdp: 16 (over z, y, core), sp: 2 (over x).
Axes of the slice: x: 2, y: 2, z: 4, core: 2. Of those that a mesh axis runs over, the one named last changes fastest.
Arguments:
- latents: bfloat16 [32, 256, 768], P('fsdp', 'sp'), may hold values from -6 to 6
- condition: bfloat16 [32, 768], P('fsdp'), may hold values from -6 to 6
- cotangent: bfloat16 [32, 256, 768], P('fsdp', 'sp'), may hold values from -6 to 6
- w_ada: bfloat16 [768, 4608], P('fsdp'), may hold values from -0.21875 to 0.21875
- b_ada: bfloat16 [4608], P('fsdp'), may hold values from -3 to 3
- w_qkv: bfloat16 [768, 2304], P('fsdp'), may hold values from -0.21875 to 0.21875
- b_query: bfloat16 [768], P('fsdp'), may hold values from -3 to 3
- b_value: bfloat16 [768], P('fsdp'), may hold values from -3 to 3
- w_out: bfloat16 [768, 768], P('fsdp'), may hold values from -0.875 to 0.875
- b_out: bfloat16 [768], P('fsdp'), may hold values from -3 to 3
- w_up: bfloat16 [768, 3072], P('fsdp'), may hold values from -0.21875 to 0.21875
- b_up: bfloat16 [3072], P('fsdp'), may hold values from -3 to 3
- w_down: bfloat16 [3072, 768], P('fsdp'), may hold values from -0.109375 to 0.109375
- b_down: bfloat16 [768], P('fsdp'), may hold values from -3 to 3
Outputs:
- output: bfloat16 [32, 256, 768], P('fsdp', 'sp')
- grad_latents: float32 [32, 256, 768], P('fsdp', 'sp')
- grad_condition: float32 [32, 768], P('fsdp')
- grad_w_ada: float32 [768, 4608], P(('fsdp', 'sp'))
- grad_b_ada: float32 [4608], P(('fsdp', 'sp'))
- grad_w_qkv: float32 [768, 2304], P(('fsdp', 'sp'))
- grad_b_query: float32 [768], P(('fsdp', 'sp'))
- grad_b_value: float32 [768], P(('fsdp', 'sp'))
- grad_w_out: float32 [768, 768], P(('fsdp', 'sp'))
- grad_b_out: float32 [768], P(('fsdp', 'sp'))
- grad_w_up: float32 [768, 3072], P(('fsdp', 'sp'))
- grad_b_up: float32 [3072], P(('fsdp', 'sp'))
- grad_w_down: float32 [3072, 768], P(('fsdp', 'sp'))
- grad_b_down: float32 [768], P(('fsdp', 'sp'))
All inputs are finite; a program needn't handle non-finite values.
Results may differ from a plain program's by a relative error of at most 0.015.
The roundings to bfloat16 on the way count: a program that leaves them out, or rounds other values in their place, can miss the bound.
Values may be sent and summed in bfloat16 or wider, within the bound.
A program may use at most 256 MiB of HBM per device.

v0:
```python
import jax
import jax.numpy as jnp
from jax import lax
from jax.sharding import PartitionSpec as P

D = 768
H = 12
HD = 64
eps = 1e-06


def normalize(values):
    centered = values - jnp.mean(values, axis=-1, keepdims=True)
    inverse = lax.rsqrt(jnp.mean(centered * centered, axis=-1, keepdims=True) + eps)
    return (centered * inverse, inverse)


def norm_back(grad_in, normed, inverse):
    return inverse * (
        grad_in
        - jnp.mean(grad_in, axis=-1, keepdims=True)
        - normed * jnp.mean(grad_in * normed, axis=-1, keepdims=True)
    )


def gelu_tanh(values):
    return jax.nn.gelu(values, approximate=True)


def silu_back(values, grad_out):
    return jax.vjp(jax.nn.silu, values)[1](grad_out)[0]


def gelu_back(values, grad_out):
    return jax.vjp(gelu_tanh, values)[1](grad_out)[0]


LANES = 2048


def body(
    latents,
    condition,
    cotangent,
    w_ada,
    b_ada,
    w_qkv,
    b_query,
    b_value,
    w_out,
    b_out,
    w_up,
    b_up,
    w_down,
    b_down,
):
    f32 = jnp.float32
    bf16 = jnp.bfloat16
    fsdp_count = lax.axis_size("fsdp")
    sp_count = lax.axis_size("sp")
    owners = fsdp_count * sp_count
    fsdp_index = lax.axis_index("fsdp")
    sp_index = lax.axis_index("sp")
    owner_index = fsdp_index * sp_count + sp_index
    pair_latents = latents.shape[0]
    own_latents = pair_latents // sp_count
    latent_total = pair_latents * fsdp_count
    tokens_all = latents.shape[1] * sp_count
    scale_factor = HD ** (-0.5)
    small = [condition.reshape(-1), b_ada, b_query, b_value, b_out, b_up, b_down]
    width = sum((part.size for part in small))
    padded = -(-width // LANES) * LANES
    small.append(jnp.zeros((padded - width,), bf16))
    small_all = lax.all_gather(
        jnp.concatenate(small).reshape(1, padded // 128, 128), "fsdp", axis=0, tiled=True
    ).reshape(fsdp_count, padded)
    pieces = []
    start = 0
    for part in small[:-1]:
        pieces.append(small_all[:, start : start + part.size].reshape(-1))
        start = start + part.size
    cond_all, ada_bias, query_bias, value_bias, out_bias, up_bias, down_bias = pieces
    cond_all = cond_all.reshape(latent_total, D).astype(f32)
    silu_all = jax.nn.silu(cond_all)
    inputs = lax.all_to_all(latents, "sp", split_axis=0, concat_axis=1, tiled=True).astype(f32)
    grad_out = lax.all_to_all(cotangent, "sp", split_axis=0, concat_axis=1, tiled=True).astype(f32)
    ada_rows = w_ada.shape[0]
    silu_mine = lax.dynamic_index_in_dim(
        silu_all.astype(bf16).reshape(fsdp_count, sp_count, own_latents, D), sp_index, 1, False
    )
    silu_mine = lax.dynamic_index_in_dim(
        silu_mine.reshape(fsdp_count * own_latents, fsdp_count, ada_rows), fsdp_index, 1, False
    )
    mod_part = jnp.dot(silu_mine, w_ada, preferred_element_type=f32)
    mod_part = lax.all_to_all(
        mod_part.reshape(fsdp_count, own_latents * 6 * D),
        "fsdp",
        split_axis=0,
        concat_axis=0,
        tiled=True,
    )
    modulate = jnp.sum(mod_part, axis=0).reshape(own_latents, 6 * D) + ada_bias.astype(f32)
    mod_parts = modulate.reshape(own_latents, 6, 1, D)
    shift_one, scale_one, gate_one = (mod_parts[:, 0], mod_parts[:, 1], mod_parts[:, 2])
    shift_two, scale_two, gate_two = (mod_parts[:, 3], mod_parts[:, 4], mod_parts[:, 5])
    qkv_full = lax.all_gather(w_qkv, "fsdp", axis=0, tiled=True)
    out_full = lax.all_gather(w_out, "fsdp", axis=0, tiled=True)
    up_full = lax.all_gather(w_up, "fsdp", axis=0, tiled=True)
    down_full = lax.all_gather(w_down, "fsdp", axis=0, tiled=True)
    normed_one, inverse_one = normalize(inputs)
    attn_in = (normed_one * (1.0 + scale_one) + shift_one).astype(bf16)
    qkv_bias = jnp.concatenate([query_bias, jnp.zeros_like(query_bias), value_bias]).astype(f32)
    projected = (
        jnp.einsum("btd,de->bte", attn_in, qkv_full, preferred_element_type=f32) + qkv_bias
    ).astype(bf16)
    heads = projected.reshape(own_latents, tokens_all, 3, H, HD).transpose(2, 0, 3, 1, 4)
    queries, key_heads, value_heads = (heads[0], heads[1], heads[2])
    scores = (
        jnp.einsum("bhqd,bhkd->bhqk", queries, key_heads, preferred_element_type=f32) * scale_factor
    )
    log_total = jnp.log(jnp.sum(jnp.exp(scores), axis=-1, keepdims=True))
    soft_float = jnp.exp(scores - log_total)
    soft_half = soft_float.astype(bf16)
    mixed = jnp.einsum(
        "bhqk,bhkd->bhqd", soft_half, value_heads, preferred_element_type=f32
    ).astype(bf16)
    mixed_tokens = mixed.transpose(0, 2, 1, 3).reshape(own_latents, tokens_all, D)
    attn_proj = jnp.einsum(
        "btd,de->bte", mixed_tokens, out_full, preferred_element_type=f32
    ) + out_bias.astype(f32)
    residual = inputs + gate_one * attn_proj
    normed_two, inverse_two = normalize(residual)
    mlp_in = (normed_two * (1.0 + scale_two) + shift_two).astype(bf16)
    up_value = jnp.einsum(
        "btd,df->btf", mlp_in, up_full, preferred_element_type=f32
    ) + up_bias.astype(f32)
    activated = gelu_tanh(up_value).astype(bf16)
    down_value = jnp.einsum(
        "btf,fd->btd", activated, down_full, preferred_element_type=f32
    ) + down_bias.astype(f32)
    output = (residual + gate_two * down_value).astype(bf16)
    output = lax.all_to_all(output, "sp", split_axis=1, concat_axis=0, tiled=True)
    grad_gate_two = jnp.sum(grad_out * down_value, axis=1)
    grad_down = (grad_out * gate_two).astype(bf16)
    gw_down = jnp.einsum("btf,btd->fd", activated, grad_down, preferred_element_type=f32)
    gb_down = jnp.sum(grad_down.astype(f32), axis=(0, 1))
    grad_act = jnp.einsum("btd,fd->btf", grad_down, down_full, preferred_element_type=f32)
    grad_up = gelu_back(up_value, grad_act).astype(bf16)
    gw_up = jnp.einsum("btd,btf->df", mlp_in, grad_up, preferred_element_type=f32)
    gb_up = jnp.sum(grad_up.astype(f32), axis=(0, 1))
    grad_mlp = jnp.einsum("btf,df->btd", grad_up, up_full, preferred_element_type=f32)
    grad_scale_two = jnp.sum(grad_mlp * normed_two, axis=1)
    grad_shift_two = jnp.sum(grad_mlp, axis=1)
    grad_resid = grad_out + norm_back(grad_mlp * (1.0 + scale_two), normed_two, inverse_two)
    grad_gate_one = jnp.sum(grad_resid * attn_proj, axis=1)
    grad_proj = (grad_resid * gate_one).astype(bf16)
    gw_out = jnp.einsum("btd,bte->de", mixed_tokens, grad_proj, preferred_element_type=f32)
    gb_out = jnp.sum(grad_proj.astype(f32), axis=(0, 1))
    grad_mixed = jnp.einsum("bte,de->btd", grad_proj, out_full, preferred_element_type=f32).astype(
        bf16
    )
    grad_heads = grad_mixed.reshape(own_latents, tokens_all, H, HD).transpose(0, 2, 1, 3)
    grad_soft = jnp.einsum("bhqd,bhkd->bhqk", grad_heads, value_heads, preferred_element_type=f32)
    delta_sum = jnp.sum(soft_float * grad_soft, axis=-1, keepdims=True)
    grad_scores = (soft_float * (grad_soft - delta_sum)).astype(bf16)
    grad_queries = (
        jnp.einsum("bhqk,bhkd->bhqd", grad_scores, key_heads, preferred_element_type=f32)
        * scale_factor
    ).astype(bf16)
    grad_keys = (
        jnp.einsum("bhqk,bhqd->bhkd", grad_scores, queries, preferred_element_type=f32)
        * scale_factor
    ).astype(bf16)
    grad_values = jnp.einsum(
        "bhqk,bhqd->bhkd", soft_half, grad_heads, preferred_element_type=f32
    ).astype(bf16)
    grad_tokens = (
        jnp.stack([grad_queries, grad_keys, grad_values], axis=0)
        .transpose(1, 3, 0, 2, 4)
        .reshape(own_latents, tokens_all, 3 * D)
    )
    gw_qkv = jnp.einsum("btd,bte->de", attn_in, grad_tokens, preferred_element_type=f32)
    grad_tok_float = grad_tokens.astype(f32)
    gb_query = jnp.sum(grad_tok_float[:, :, :D], axis=(0, 1))
    gb_value = jnp.sum(grad_tok_float[:, :, 2 * D :], axis=(0, 1))
    grad_attn_in = jnp.einsum("bte,de->btd", grad_tokens, qkv_full, preferred_element_type=f32)
    grad_scale_one = jnp.sum(grad_attn_in * normed_one, axis=1)
    grad_shift_one = jnp.sum(grad_attn_in, axis=1)
    grad_latents = grad_resid + norm_back(grad_attn_in * (1.0 + scale_one), normed_one, inverse_one)
    grad_latents = lax.all_to_all(grad_latents, "sp", split_axis=1, concat_axis=0, tiled=True)
    grad_mod = jnp.concatenate(
        [
            grad_shift_one,
            grad_scale_one,
            grad_gate_one,
            grad_shift_two,
            grad_scale_two,
            grad_gate_two,
        ],
        axis=1,
    )
    grad_mod = lax.all_to_all(
        jnp.broadcast_to(grad_mod[None], (owners, own_latents, 6 * D)),
        ("fsdp", "sp"),
        split_axis=0,
        concat_axis=0,
        tiled=True,
    ).reshape(latent_total, 6 * D)
    rows = D // owners
    biases = (gb_query, gb_value, gb_out, gb_up, gb_down)
    bias_rows = jnp.concatenate([part.reshape(owners, -1) for part in biases], axis=1)
    bias_width = bias_rows.shape[1]
    bias_lanes = -(-bias_width // (rows * 128)) * 128
    bias_rows = jnp.pad(bias_rows, ((0, 0), (0, rows * bias_lanes - bias_width)))
    stack = down_full.shape[0] // D
    gw_down = (
        gw_down.astype(bf16)
        .reshape(owners, stack, rows, D)
        .transpose(0, 2, 1, 3)
        .reshape(D, stack * D)
    )
    packed = jnp.concatenate(
        [
            gw_down,
            gw_up.astype(bf16),
            gw_qkv.astype(bf16),
            gw_out.astype(bf16),
            bias_rows.astype(bf16).reshape(D, bias_lanes),
        ],
        axis=1,
    )
    owned = lax.psum_scatter(packed, ("fsdp", "sp"), scatter_dimension=0, tiled=True).astype(f32)
    own_weights = []
    start = 0
    for width in (stack * D, up_full.shape[1], 3 * D, D, bias_lanes):
        own_weights.append(owned[:, start : start + width])
        start = start + width
    own_down, own_up, own_qkv, own_out, bias_sums = own_weights
    own_down = own_down.reshape(rows, stack, D).transpose(1, 0, 2).reshape(stack * rows, D)
    bias_sums = bias_sums.reshape(-1)
    own_bias = []
    start = 0
    for part in biases:
        width = part.size // owners
        own_bias.append(bias_sums[start : start + width])
        start = start + width
    own_gb_query, own_gb_value, own_gb_out, own_gb_up, own_gb_down = own_bias
    silu_rows = lax.dynamic_index_in_dim(
        silu_all.reshape(latent_total, owners, D // owners), owner_index, 1, False
    )
    own_ada = jnp.dot(silu_rows.T, grad_mod, precision=lax.Precision.HIGHEST)
    own_gb_ada = lax.dynamic_index_in_dim(
        jnp.sum(grad_mod, axis=0).reshape(owners, -1), owner_index, 0, False
    )
    grad_silu = jnp.dot(grad_mod.astype(bf16), w_ada.T, preferred_element_type=f32)
    grad_silu = lax.all_to_all(
        grad_silu.reshape(fsdp_count, pair_latents * ada_rows),
        "fsdp",
        split_axis=0,
        concat_axis=0,
        tiled=True,
    )
    grad_silu = (
        grad_silu.reshape(fsdp_count, pair_latents, ada_rows)
        .transpose(1, 0, 2)
        .reshape(pair_latents, D)
    )
    grad_condition = silu_back(condition.astype(f32), grad_silu)
    return (
        output,
        grad_latents,
        grad_condition,
        own_ada,
        own_gb_ada,
        own_qkv,
        own_gb_query,
        own_gb_value,
        own_out,
        own_gb_out,
        own_up,
        own_gb_up,
        own_down,
        own_gb_down,
    )


def solution(mesh):
    in_specs = (
        P("fsdp", "sp", None),
        P("fsdp", None),
        P("fsdp", "sp", None),
        P("fsdp", None),
        P("fsdp"),
        P("fsdp", None),
        P("fsdp"),
        P("fsdp"),
        P("fsdp", None),
        P("fsdp"),
        P("fsdp", None),
        P("fsdp"),
        P("fsdp", None),
        P("fsdp"),
    )
    out_specs = (
        P("fsdp", "sp", None),
        P("fsdp", "sp", None),
        P("fsdp", None),
        P(("fsdp", "sp"), None),
        P(("fsdp", "sp")),
        P(("fsdp", "sp"), None),
        P(("fsdp", "sp")),
        P(("fsdp", "sp")),
        P(("fsdp", "sp"), None),
        P(("fsdp", "sp")),
        P(("fsdp", "sp"), None),
        P(("fsdp", "sp")),
        P(("fsdp", "sp"), None),
        P(("fsdp", "sp")),
    )
    return jax.shard_map(body, mesh=mesh, in_specs=in_specs, out_specs=out_specs, check_vma=False)
```

profile of v0, /device:TPU:0, one launch (start us, length us, event | category | flops | bytes accessed | tf_op | source)
XLA Modules:
  0.0 443.4 jit_solution(5523221434767197551)
XLA Ops:
  10.0 4.2 all-to-all-start
  14.9 4.1 concatenate.24
  19.1 22.7 %all_gather.15 = bf16[16,32,128]{2,1,0:T(8,128)(2,1)S(1)} all-gather(bf16[1,32,128]{2,1,0:T(8,128)(2,1)S(1)} %bitcast.188), channel_id=1, replica_groups=mesh['fsdp'=16,'sp'=2] {'fsdp'}, dimensions={0}, use_global_device_ids=true | all-gather | bytes 139264 | tf_op jit(solution)/shard_map/all_gather | solution.py:74
  43.7 3.5 all-to-all-start.1
  48.0 13.7 %all-to-all-done.1 = f32[16,1,4608]{2,1,0:T(1,128)S(1)} async-done(((f32[16,1,4608]{2,1,0:T(1,128)}), f32[16,1,4608]{2,1,0:T(1,128)S(1)}, u32[]{:S(2)}, u32[]{:S(2)}) %all-to-all-start.1) | async-done | bytes 294944 | tf_op jit(solution)/shard_map/all_to_all | solution.py:95
  61.7 3.8 all-to-all-start.3
  65.8 6.4 %all-to-all-done.3 = bf16[2,128,768]{2,1,0:T(8,128)(2,1)S(1)} async-done(((bf16[2,128,768]{2,1,0:T(8,128)(2,1)}), bf16[2,128,768]{2,1,0:T(8,128)(2,1)S(1)}, u32[]{:S(2)}, u32[]{:S(2)}) %all-to-all-start.3) | async-done | bytes 393248 | tf_op jit(solution)/shard_map/all_to_all | solution.py:86
  74.5 4.1 fusion.3
  78.6 1.6 copy.105
  80.2 2.4 fusion.60
  82.6 4.9 %convolution_convert_fusion.4 = bf16[12,256,64]{1,2,0:T(8,128)(2,1)} fusion(f32[12,256,256]{1,2,0:T(8,128)} %fusion.60, bf16[3,1,12,256,64]{3,4,2,1,0:T(8,128)(2,1)S(1)} %bitcast.160), kind=kOutput, calls=%fused_computation.34 | convolution fusion | flops 104008960 | bytes 7077888 | tf_op jit(solution)/shard_map/bhqk,bhkd->bhqd/dot_general | solution.py:124
  87.4 17.1 %all-gather.7.cloned.1.call-done = bf16[768,768]{1,0:T(8,128)(2,1)} async-done(((bf16[48,768]{1,0:T(8,128)(2,1)}), bf16[768,768]{1,0:T(8,128)(2,1)}) %all-gather.7.cloned.1.call-update) | async-done | bytes 1179664 | tf_op jit(solution)/shard_map/all_gather | solution.py:107
  104.6 2.8 fusion.83
  107.6 51.3 %all-gather.11.cloned.1.call-done = bf16[3072,768]{1,0:T(8,128)(2,1)} async-done(((bf16[192,768]{1,0:T(8,128)(2,1)}), bf16[3072,768]{1,0:T(8,128)(2,1)}) %all-gather.11.cloned.1.call-update) | async-done | bytes 4718608 | tf_op jit(solution)/shard_map/all_gather | solution.py:109
  158.9 5.6 %fusion.86 = f32[256,3072]{1,0:T(8,128)} fusion(bf16[256,768]{1,0:T(8,128)(2,1)} %fusion.24, bf16[3072,768]{1,0:T(8,128)(2,1)} %all-gather.11.cloned.1.call-done), kind=kOutput, calls=%fused_computation.159 | convolution fusion | flops 1207959552 | bytes 8257536 | tf_op jit(solution)/shard_map/btd,fd->btf/dot_general | solution.py:147
  164.5 48.2 %all-gather.9.cloned.1.call-done = bf16[768,3072]{1,0:T(8,128)(2,1)} async-done(((bf16[48,3072]{1,0:T(8,128)(2,1)}), bf16[768,3072]{1,0:T(8,128)(2,1)}) %all-gather.9.cloned.1.call-update) | async-done | bytes 4718608 | tf_op jit(solution)/shard_map/all_gather | solution.py:108
  212.7 7.0 %fusion.80 = (bf16[3072]{0:T(1024)(128)(2,1)S(1)}, bf16[256,3072]{1,0:T(8,128)(2,1)S(1)}, f32[256,3072]{1,0:T(8,128)S(1)}) fusion(f32[256,3072]{1,0:T(8,128)} %fusion.86, f32[3072]{0:T(1024)S(1)} %reshape.760, bf16[768,3072]{1,0:T(8,128)(2,1)} %all-gather.9.cloned.1.call-done, f32[256,768]{1,0:T(8,128)S(1)} %get-tuple-element.36, ...), kind=kOutput, calls=%fused_computation.153 | convolution fusion | flops 1226241024 | bytes 13395968 | tf_op jit(solution)/shard_map/btd,df->btf/dot_general | solution.py:134
  219.8 1.4 fusion.87
  222.1 1.7 copy-done.2
  223.8 2.9 fusion.25
  226.7 1.3 fusion.82
  230.2 5.0 %fusion.20 = bf16[1,1,12,256,64]{3,4,2,1,0:T(8,128)(2,1)} fusion(bf16[12,256,64]{1,2,0:T(8,128)(2,1)} %bitcast.174, f32[12,256,256]{1,2,0:T(8,128)} %fusion.60), kind=kOutput, calls=%fused_computation.39 | convolution fusion | flops 104008960 | bytes 3932160 | tf_op jit(solution)/shard_map/bhqk,bhqd->bhkd/dot_general | solution.py:174
  235.8 1.3 copy-done.1
  237.1 2.9 multiply_reduce_fusion
  240.6 1.4 fusion.22
  241.9 1.1 fusion.21
  243.1 4.4 convolution_convert_fusion.2
  247.7 1.2 pad_maximum_fusion
  249.8 4.7 %copy.117 = bf16[32,24,4,768]{3,2,1,0:T(4,128)(2,1)S(1)} copy(bf16[32,24,4,768]{3,1,2,0:T(8,128)(2,1)} %bitcast.167) | data formatting | bytes 9437184 | tf_op jit(solution)/shard_map/transpose | solution.py:219
  255.6 2.5 constant_dynamic-update-slice_fusion.7
  258.0 3.7 fusion.2
  261.8 2.9 fusion.1
  264.7 1.6 fusion.17
  269.1 3.3 reduce.65
  273.2 3.6 all-to-all-start.2
  276.8 3.9 fusion.39
  281.1 1.7 copy.113
  282.8 1.2 all-to-all-done.2
  284.0 3.6 all-to-all-start.4
  287.7 10.6 %all-to-all-done.4 = f32[1,256,768]{2,0,1:T(1,128)S(1)} async-done(((f32[1,256,768]{2,0,1:T(1,128)}), f32[1,256,768]{2,0,1:T(1,128)S(1)}, u32[]{:S(2)}, u32[]{:S(2)}) %all-to-all-start.4) | async-done | bytes 786464 | tf_op jit(solution)/shard_map/all_to_all | solution.py:190
  299.4 2.6 all-to-all-start.5
  304.5 18.4 %all-to-all-done.5 = f32[32,1,4608]{2,1,0:T(1,128)S(1)} async-done(((f32[32,1,4608]{2,1,0:T(1,128)}), f32[32,1,4608]{2,1,0:T(1,128)S(1)}, u32[]{:S(2)}, u32[]{:S(2)}) %all-to-all-start.5) | async-done | bytes 589856 | tf_op jit(solution)/shard_map/all_to_all | solution.py:202
  323.9 3.5 all-to-all-start.6
  327.8 1.3 fusion.46
  329.7 6.0 %all-to-all-done.6 = f32[16,1,96]{2,1,0:T(1,128)S(1)} async-done(((f32[16,1,96]{2,1,0:T(1,128)}), f32[16,1,96]{2,1,0:T(1,128)S(1)}, u32[]{:S(2)}, u32[]{:S(2)}) %all-to-all-start.6) | async-done | bytes 6176 | tf_op jit(solution)/shard_map/all_to_all | solution.py:256
  337.6 92.9 %reduce-scatter.4.cloned.1.call-done = bf16[24,9344]{1,0:T(8,128)(2,1)} async-done(((bf16[768,9344]{1,0:T(8,128)(2,1)}), bf16[24,9344]{1,0:T(8,128)(2,1)}) %reduce-scatter.4.cloned.1.call-update) | async-done | bytes 448528
  430.5 1.1 convert_element_type.313
  432.8 1.7 fusion.84
  (144 shorter events, 30.4 us)
Async XLA Ops:
  7.2 35.3 %copy-start = (bf16[48,4608]{1,0:T(8,128)(2,1)S(1)}, bf16[48,4608]{1,0:T(8,128)(2,1)}, u32[]{:S(2)}) copy-start(bf16[48,4608]{1,0:T(8,128)(2,1)} %param.17) | copy-start | bytes 1327108
  7.2 67.3 %all-gather.5.cloned.1.call-start = ((), (), s32[]{:S(2)}) async-start(), calls=%async_computation.8 | async-start | bytes 3760128 | tf_op jit(solution)/shard_map/all_gather | solution.py:106
  7.9 96.6 %all-gather.7.cloned.1.call-start = ((), (), s32[]{:S(2)}) async-start(), calls=%async_computation.9 | async-start | bytes 1253376 | tf_op jit(solution)/shard_map/all_gather | solution.py:107
  8.7 150.2 %all-gather.11.cloned.1.call-start = ((), (), s32[]{:S(2)}) async-start(), calls=%async_computation.11 | async-start | bytes 5013504 | tf_op jit(solution)/shard_map/all_gather | solution.py:109
  9.4 203.3 %all-gather.9.cloned.1.call-start = ((), (), s32[]{:S(2)}) async-start(), calls=%async_computation.10 | async-start | bytes 5013504 | tf_op jit(solution)/shard_map/all_gather | solution.py:108
  10.0 33.7 %all-to-all-start = ((bf16[2,128,768]{2,1,0:T(8,128)(2,1)}), bf16[2,128,768]{2,1,0:T(8,128)(2,1)S(1)}, u32[]{:S(2)}, u32[]{:S(2)}) async-start(bf16[2,128,768]{2,1,0:T(8,128)(2,1)} %param.14), calls=%async_computation | async-start | bytes 786432 | tf_op jit(solution)/shard_map/all_to_all | solution.py:85
  43.7 18.0 %all-to-all-start.1 = ((f32[16,1,4608]{2,1,0:T(1,128)}), f32[16,1,4608]{2,1,0:T(1,128)S(1)}, u32[]{:S(2)}, u32[]{:S(2)}) async-start(f32[16,1,4608]{2,1,0:T(1,128)} %copy.104), calls=%async_computation.1 | async-start | bytes 589824 | tf_op jit(solution)/shard_map/all_to_all | solution.py:95
  61.7 10.5 %all-to-all-start.3 = ((bf16[2,128,768]{2,1,0:T(8,128)(2,1)}), bf16[2,128,768]{2,1,0:T(8,128)(2,1)S(1)}, u32[]{:S(2)}, u32[]{:S(2)}) async-start(bf16[2,128,768]{2,1,0:T(8,128)(2,1)} %param.16), calls=%async_computation.3 | async-start | bytes 786432 | tf_op jit(solution)/shard_map/all_to_all | solution.py:86
  65.5 365.0 %reduce-scatter.4.cloned.1.call-start = ((), (), s32[]{:S(2)}) async-start(), calls=%async_computation.12 | async-start | bytes 14800896
  212.7 7.0 %copy-start.16 = (bf16[768,3072]{1,0:T(8,128)(2,1)S(1)}, bf16[768,3072]{1,0:T(8,128)(2,1)}, u32[]{:S(2)}) copy-start(bf16[768,3072]{1,0:T(8,128)(2,1)} %all-gather.9.cloned.1.call-done) | copy-start | bytes 14155780
  219.7 1.5 copy-start.17
  219.8 2.4 copy-start.19
  219.8 4.0 copy-start.2
  226.7 2.0 copy-start.3
  228.0 0.8 copy-start.5
  230.2 5.0 %copy-start.12 = (bf16[256,768]{0,1:T(8,128)(2,1)S(1)}, bf16[256,768]{0,1:T(8,128)(2,1)}, u32[]{:S(2)}) copy-start(bf16[256,768]{0,1:T(8,128)(2,1)} %copy.109) | copy-start | bytes 1179652
  235.2 1.9 copy-start.1
  240.5 2.5 copy-start.9
  240.6 2.5 copy-start.20
  243.1 4.6 %copy-start.10 = (bf16[1,1,12,256,64]{3,4,2,1,0:T(8,128)(2,1)S(1)}, bf16[1,1,12,256,64]{3,4,2,1,0:T(8,128)(2,1)}, u32[]{:S(2)}) copy-start(bf16[1,1,12,256,64]{3,4,2,1,0:T(8,128)(2,1)} %fusion.22) | copy-start | bytes 1179652
  255.6 2.5 copy-start.18
  258.0 3.7 copy-start.13
  261.8 2.9 copy-start.6
  261.8 2.9 copy-start.11
  267.0 1.0 copy-start.14
  273.2 10.8 %all-to-all-start.2 = ((bf16[2,2,49152]{2,1,0:T(2,128)(2,1)}), bf16[2,2,49152]{2,1,0:T(2,128)(2,1)S(1)}, u32[]{:S(2)}, u32[]{:S(2)}) async-start(bf16[2,2,49152]{2,1,0:T(2,128)(2,1)} %reshape.781), calls=%async_computation.2 | async-start | bytes 786432 | tf_op jit(solution)/shard_map/all_to_all | solution.py:142
  276.8 4.0 copy-start.7
  276.8 4.0 copy-start.8
  284.0 14.2 %all-to-all-start.4 = ((f32[1,256,768]{2,0,1:T(1,128)}), f32[1,256,768]{2,0,1:T(1,128)S(1)}, u32[]{:S(2)}, u32[]{:S(2)}) async-start(f32[1,256,768]{2,0,1:T(1,128)} %copy.113), calls=%async_computation.4 | async-start | bytes 1572864 | tf_op jit(solution)/shard_map/all_to_all | solution.py:190
  299.4 23.6 %all-to-all-start.5 = ((f32[32,1,4608]{2,1,0:T(1,128)}), f32[32,1,4608]{2,1,0:T(1,128)S(1)}, u32[]{:S(2)}, u32[]{:S(2)}) async-start(f32[32,1,4608]{2,1,0:T(1,128)} %broadcast_in_dim.11), calls=%async_computation.5 | async-start | bytes 1179648 | tf_op jit(solution)/shard_map/all_to_all | solution.py:202
  302.4 34.6 %copy-start.15 = (bf16[2,768]{1,0:T(2,128)(2,1)S(1)}, bf16[2,768]{1,0:T(2,128)(2,1)}, u32[]{:S(2)}) copy-start(bf16[2,768]{1,0:T(2,128)(2,1)} %param.15) | copy-start | bytes 9220
  323.9 11.8 %all-to-all-start.6 = ((f32[16,1,96]{2,1,0:T(1,128)}), f32[16,1,96]{2,1,0:T(1,128)S(1)}, u32[]{:S(2)}, u32[]{:S(2)}) async-start(f32[16,1,96]{2,1,0:T(1,128)} %bitcast.29), calls=%async_computation.6 | async-start | bytes 16384 | tf_op jit(solution)/shard_map/all_to_all | solution.py:256
  430.5 5.0 %copy-start.4 = (bf16[24,9344]{1,0:T(8,128)(2,1)S(1)}, bf16[24,9344]{1,0:T(8,128)(2,1)}, u32[]{:S(2)}) copy-start(bf16[24,9344]{1,0:T(8,128)(2,1)} %reduce-scatter.4.cloned.1.call-done) | copy-start | bytes 1345540
Sparse Core Ops, SparseCore 0:
  10.3 55.0 all-gather.4
  67.7 36.8 all-gather.6
  106.9 51.9 all-gather.10
  161.0 51.6 all-gather.8
  267.1 163.3 reduce-scatter.3
where the time goes:
time: 444 us; the launch traced here: 443 us
  waiting for transfers between devices  268 us (60%)
  matrix products  58 us (13%)
  local copies, waits for them, and re-layouts  38.8 us (9%)
  starting transfers between devices  24.9 us (6%)
  blocking collectives  22.7 us (5%)
  other arithmetic  16.2 us (4%)
  between operations  14.4 us (3%)
    unnamed x6, waiting for transfers between devices  95.5 us
    all_gather x1, waiting for transfers between devices, body(): down_full = lax.all_gather(w_down, 'fsdp', axis=0, tiled=True)  51.3 us
    all_gather x1, waiting for transfers between devices, body(): up_full = lax.all_gather(w_up, 'fsdp', axis=0, tiled=True)  48.2 us
    all_gather x1, blocking collectives, body(): lax.all_gather(jnp.concatenate(small).reshape(1, padded // 128, 128), 'fs...  22.7 us
    all_to_all x1, waiting for transfers between devices, body(): lax.all_to_all(jnp.broadcast_to(grad_mod[None], (owners, own_latents, 6 *...  18.4 us
    all_gather x1, waiting for transfers between devices, body(): out_full = lax.all_gather(w_out, 'fsdp', axis=0, tiled=True)  17.1 us
    all_to_all x1, waiting for transfers between devices, body(): lax.all_to_all(mod_part.reshape(fsdp_count, own_latents * 6 * D), 'fsdp',...  13.7 us
    unnamed x55, local copies, waits for them, and re-layouts  12.7 us
  transfers between devices with their start and end apart: 12, of which 10 were waited for; matrix products, arithmetic and copies ran while one was open for 12% of the time, Pallas kernels for 0%

commit v1 on v0

--- a/solution.py
+++ b/solution.py
@@ -7,6 +7,14 @@
 H = 12
 HD = 64
 eps = 1e-06
+
+
+def report_values_over_axis(inp, arr_in):
+    return jnp.split(
+        lax.all_gather(jnp.concatenate([arr_in, inp], 1), "fsdp", axis=0, tiled=True),
+        [arr_in.shape[1]],
+        1,
+    )
 
 
 def normalize(values):
@@ -104,8 +112,7 @@
     shift_one, scale_one, gate_one = (mod_parts[:, 0], mod_parts[:, 1], mod_parts[:, 2])
     shift_two, scale_two, gate_two = (mod_parts[:, 3], mod_parts[:, 4], mod_parts[:, 5])
     qkv_full = lax.all_gather(w_qkv, "fsdp", axis=0, tiled=True)
-    out_full = lax.all_gather(w_out, "fsdp", axis=0, tiled=True)
-    up_full = lax.all_gather(w_up, "fsdp", axis=0, tiled=True)
+    out_full, up_full = report_values_over_axis(w_up, w_out)
     down_full = lax.all_gather(w_down, "fsdp", axis=0, tiled=True)
     normed_one, inverse_one = normalize(inputs)
     attn_in = (normed_one * (1.0 + scale_one) + shift_one).astype(bf16)

time: 444 us -> 412 us (0.928)
  waiting for transfers between devices: 268 us -> 235 us
    all_gather x1, waiting for transfers between devices: 51.3 us -> 32.3 us  [body(): down_full = lax.all_gather(w_down, 'fsdp', axis=0, tiled=True)]
    all_gather x2 -> x1, waiting for transfers between devices: 65.3 us -> 55.2 us  [report_values_over_axis(): lax.all_gather(jnp.concatenate([arr_in, inp], 1), 'fsdp', axis=0, tiled=T...]
    unnamed x6 -> x5, waiting for transfers between devices: 95.5 us -> 91.6 us
    unnamed x55 -> x59, local copies, waits for them, and re-layouts: 12.7 us -> 14.8 us
  transfers between devices with their start and end apart: 12 -> 11, of which waited for: 10 -> 9; matrix products, arithmetic and copies ran while one was open for 12% -> 12% of each run, Pallas kernels for 0% -> 0%
where the time goes in v1:
time: 412 us; the launch traced here: 411 us
  waiting for transfers between devices  235 us (57%)
  matrix products  57 us (14%)
  local copies, waits for them, and re-layouts  41.1 us (10%)
  starting transfers between devices  25.3 us (6%)
  blocking collectives  22.7 us (6%)
  other arithmetic  15.7 us (4%)
  between operations  14.4 us (3%)
    unnamed x5, waiting for transfers between devices  91.6 us
    all_gather x1, waiting for transfers between devices, report_values_over_axis(): lax.all_gather(jnp.concatenate([arr_in, inp], 1), 'fsdp', axis=0, tiled=T...  55.2 us
    all_gather x1, waiting for transfers between devices, body(): down_full = lax.all_gather(w_down, 'fsdp', axis=0, tiled=True)  32.3 us
    all_gather x1, blocking collectives, body(): lax.all_gather(jnp.concatenate(small).reshape(1, padded // 128, 128), 'fs...  22.7 us
    all_to_all x1, waiting for transfers between devices, body(): lax.all_to_all(jnp.broadcast_to(grad_mod[None], (owners, own_latents, 6 *...  18.8 us
    unnamed x59, local copies, waits for them, and re-layouts  14.8 us
    all_to_all x1, waiting for transfers between devices, body(): lax.all_to_all(mod_part.reshape(fsdp_count, own_latents * 6 * D), 'fsdp',...  13.9 us
    all_to_all x1, waiting for transfers between devices, body(): lax.all_to_all(grad_latents, 'sp', split_axis=1, concat_axis=0, tiled=True)  10.5 us
  transfers between devices with their start and end apart: 11, of which 9 were waited for; matrix products, arithmetic and copies ran while one was open for 12% of the time, Pallas kernels for 0%

profile of v1, /device:TPU:0, one launch (start us, length us, event | category | flops | bytes accessed | tf_op | source)
XLA Modules:
  0.0 411.2 jit_solution(12734463641116236920)
XLA Ops:
  8.7 1.7 pad_maximum_fusion.1
  10.5 4.2 %all-to-all-start = ((bf16[2,128,768]{2,1,0:T(8,128)(2,1)}), bf16[2,128,768]{2,1,0:T(8,128)(2,1)S(1)}, u32[]{:S(2)}, u32[]{:S(2)}) async-start(bf16[2,128,768]{2,1,0:T(8,128)(2,1)} %param.14), calls=%async_computation | async-start | bytes 786432 | tf_op jit(solution)/shard_map/all_to_all | solution.py:93
  15.4 4.1 concatenate.27
  19.5 22.7 %all_gather.12 = bf16[16,32,128]{2,1,0:T(8,128)(2,1)S(1)} all-gather(bf16[1,32,128]{2,1,0:T(8,128)(2,1)S(1)} %bitcast.188), channel_id=1, replica_groups=mesh['fsdp'=16,'sp'=2] {'fsdp'}, dimensions={0}, use_global_device_ids=true | all-gather | bytes 139264 | tf_op jit(solution)/shard_map/all_gather | solution.py:82
  44.2 3.5 all-to-all-start.1
  48.5 13.9 %all-to-all-done.1 = f32[16,1,4608]{2,1,0:T(1,128)S(1)} async-done(((f32[16,1,4608]{2,1,0:T(1,128)}), f32[16,1,4608]{2,1,0:T(1,128)S(1)}, u32[]{:S(2)}, u32[]{:S(2)}) %all-to-all-start.1) | async-done | bytes 294944 | tf_op jit(solution)/shard_map/all_to_all | solution.py:103
  62.4 4.0 all-to-all-start.3
  66.7 6.4 %all-to-all-done.3 = bf16[2,128,768]{2,1,0:T(8,128)(2,1)S(1)} async-done(((bf16[2,128,768]{2,1,0:T(8,128)(2,1)}), bf16[2,128,768]{2,1,0:T(8,128)(2,1)S(1)}, u32[]{:S(2)}, u32[]{:S(2)}) %all-to-all-start.3) | async-done | bytes 393248 | tf_op jit(solution)/shard_map/all_to_all | solution.py:94
  74.7 4.2 %fusion.10 = bf16[256,2304]{1,0:T(8,128)(2,1)} fusion(bf16[256,768]{1,0:T(8,128)(2,1)S(1)} %fusion.43, bf16[768,2304]{1,0:T(8,128)(2,1)} %all-gather.4.cloned.1.call-done, f32[2304]{0:T(1024)S(1)} %maximum_convert_fusion), kind=kOutput, calls=%fused_computation.15 | convolution fusion | flops 907149312 | bytes 5121024 | tf_op jit(solution)/shard_map/btd,de->bte/dot_general | solution.py:121
  78.9 1.6 copy.105
  80.5 2.3 fusion.69
  82.7 4.8 %convolution_convert_fusion.4 = bf16[12,256,64]{1,2,0:T(8,128)(2,1)} fusion(f32[12,256,256]{1,2,0:T(8,128)} %fusion.69, bf16[3,1,12,256,64]{3,4,2,1,0:T(8,128)(2,1)S(1)} %bitcast.156), kind=kOutput, calls=%fused_computation.38 | convolution fusion | flops 104008960 | bytes 7077888 | tf_op jit(solution)/shard_map/bhqk,bhkd->bhqd/dot_general | solution.py:131
  87.5 32.3 %all-gather.8.cloned.1.call-done = bf16[3072,768]{1,0:T(8,128)(2,1)} async-done(((bf16[192,768]{1,0:T(8,128)(2,1)}), bf16[3072,768]{1,0:T(8,128)(2,1)}) %all-gather.8.cloned.1.call-update) | async-done | bytes 4718608 | tf_op jit(solution)/shard_map/all_gather | solution.py:116
  119.8 5.5 %fusion.95 = f32[256,3072]{1,0:T(8,128)} fusion(bf16[256,768]{1,0:T(8,128)(2,1)S(1)} %fusion.33, bf16[3072,768]{1,0:T(8,128)(2,1)} %all-gather.8.cloned.1.call-done), kind=kOutput, calls=%fused_computation.166 | convolution fusion | flops 1207959552 | bytes 8257536 | tf_op jit(solution)/shard_map/btd,fd->btf/dot_general | solution.py:154
  125.3 55.2 %all-gather.6.cloned.1.call-done = bf16[768,3840]{1,0:T(8,128)(2,1)} async-done(((bf16[48,3840]{1,0:T(8,128)(2,1)}), bf16[768,3840]{1,0:T(8,128)(2,1)}) %all-gather.6.cloned.1.call-update) | async-done | bytes 5898256 | tf_op jit(solution)/shard_map/all_gather | solution.py:14
  180.6 2.9 fusion.92
  183.8 5.5 %fusion.89 = (bf16[3072]{0:T(1024)(128)(2,1)S(1)}, bf16[256,3072]{1,0:T(8,128)(2,1)S(1)}, f32[256,3072]{1,0:T(8,128)S(1)}) fusion(f32[256,3072]{1,0:T(8,128)S(1)} %copy-done.3, f32[3072]{0:T(1024)S(1)} %reshape.760, bf16[768,3840]{1,0:T(8,128)(2,1)} %all-gather.6.cloned.1.call-done, f32[256,768]{1,0:T(8,128)S(1)} %get-tuple-element.36, ...), kind=kOutput, calls=%fused_computation.160 | convolution fusion | flops 1226241024 | bytes 13395968 | tf_op jit(solution)/shard_map/btd,df->btf/dot_general | solution.py:141
  189.4 4.5 %convolution_convert_fusion.2 = bf16[3072,768]{1,0:T(8,128)(2,1)} fusion(bf16[256,768]{1,0:T(8,128)(2,1)S(1)} %copy-done.7, f32[256,3072]{1,0:T(8,128)S(1)} %get-tuple-element.60), kind=kOutput, calls=%fused_computation.5 | convolution fusion | flops 1217396736 | bytes 8257536 | tf_op jit(solution)/shard_map/btf,btd->fd/dot_general | solution.py:152
  193.9 1.4 fusion.3
  195.3 3.0 fusion.34
  198.3 1.3 fusion.91
  200.3 1.3 convolution_convert_fusion.6
  201.6 1.2 copy.109
  202.7 4.7 %fusion.27 = bf16[1,1,12,256,64]{3,4,2,1,0:T(8,128)(2,1)} fusion(bf16[12,256,64]{1,2,0:T(8,128)(2,1)S(1)} %bitcast.172, f32[12,256,256]{1,2,0:T(8,128)} %fusion.69), kind=kOutput, calls=%fused_computation.43 | convolution fusion | flops 104008960 | bytes 3932160 | tf_op jit(solution)/shard_map/bhqk,bhqd->bhkd/dot_general | solution.py:181
  208.1 1.3 copy-done.1
  209.4 2.6 multiply_reduce_fusion
  212.6 1.3 fusion.29
  214.0 1.1 fusion.28
  215.3 4.7 %copy.117 = bf16[32,24,4,768]{3,2,1,0:T(4,128)(2,1)S(1)} copy(bf16[32,24,4,768]{3,1,2,0:T(8,128)(2,1)} %bitcast.163) | data formatting | bytes 9437184 | tf_op jit(solution)/shard_map/transpose | solution.py:226
  220.0 3.2 copy.132
  224.3 5.0 %constant_dynamic-update-slice_fusion.7 = bf16[768,9344]{1,0:T(8,128)(2,1)} fusion(bf16[768,3072]{1,0:T(8,128)(2,1)} %bitcast.153), kind=kLoop, calls=%fused_computation.116 | loop fusion | bytes 9437184
  229.2 3.8 fusion.2
  233.0 3.0 fusion.1
  236.0 1.5 fusion.24
  240.3 3.0 reduce.65
  244.2 3.7 all-to-all-start.2
  248.0 3.8 fusion.48
  252.2 1.7 copy.113
  254.9 3.6 all-to-all-start.4
  258.6 10.5 %all-to-all-done.4 = f32[1,256,768]{2,0,1:T(1,128)S(1)} async-done(((f32[1,256,768]{2,0,1:T(1,128)}), f32[1,256,768]{2,0,1:T(1,128)S(1)}, u32[]{:S(2)}, u32[]{:S(2)}) %all-to-all-start.4) | async-done | bytes 786464 | tf_op jit(solution)/shard_map/all_to_all | solution.py:197
  270.2 2.6 all-to-all-start.5
  275.4 18.8 %all-to-all-done.5 = f32[32,1,4608]{2,1,0:T(1,128)S(1)} async-done(((f32[32,1,4608]{2,1,0:T(1,128)}), f32[32,1,4608]{2,1,0:T(1,128)S(1)}, u32[]{:S(2)}, u32[]{:S(2)}) %all-to-all-start.5) | async-done | bytes 589856 | tf_op jit(solution)/shard_map/all_to_all | solution.py:209
  295.1 3.5 all-to-all-start.6
  299.0 1.3 fusion.55
  300.9 5.3 %all-to-all-done.6 = f32[16,1,96]{2,1,0:T(1,128)S(1)} async-done(((f32[16,1,96]{2,1,0:T(1,128)}), f32[16,1,96]{2,1,0:T(1,128)S(1)}, u32[]{:S(2)}, u32[]{:S(2)}) %all-to-all-start.6) | async-done | bytes 6176 | tf_op jit(solution)/shard_map/all_to_all | solution.py:263
  308.2 90.2 %reduce-scatter.4.cloned.1.call-done = bf16[24,9344]{1,0:T(8,128)(2,1)} async-done(((bf16[768,9344]{1,0:T(8,128)(2,1)}), bf16[24,9344]{1,0:T(8,128)(2,1)}) %reduce-scatter.4.cloned.1.call-update) | async-done | bytes 448528
  398.3 1.1 convert_element_type.313
  400.7 1.7 fusion.93
  (148 shorter events, 26.2 us)
Async XLA Ops:
  7.2 35.7 %copy-start = (bf16[48,4608]{1,0:T(8,128)(2,1)S(1)}, bf16[48,4608]{1,0:T(8,128)(2,1)}, u32[]{:S(2)}) copy-start(bf16[48,4608]{1,0:T(8,128)(2,1)} %param.17) | copy-start | bytes 1327108
  7.2 67.5 %all-gather.4.cloned.1.call-start = ((), (), s32[]{:S(2)}) async-start(), calls=%async_computation.8 | async-start | bytes 3760128 | tf_op jit(solution)/shard_map/all_gather | solution.py:114
  7.9 111.9 %all-gather.8.cloned.1.call-start = ((), (), s32[]{:S(2)}) async-start(), calls=%async_computation.10 | async-start | bytes 5013504 | tf_op jit(solution)/shard_map/all_gather | solution.py:116
  8.7 171.9 %all-gather.6.cloned.1.call-start = ((), (), s32[]{:S(2)}) async-start(), calls=%async_computation.9 | async-start | bytes 6266880 | tf_op jit(solution)/shard_map/all_gather | solution.py:14
  10.5 33.7 %all-to-all-start = ((bf16[2,128,768]{2,1,0:T(8,128)(2,1)}), bf16[2,128,768]{2,1,0:T(8,128)(2,1)S(1)}, u32[]{:S(2)}, u32[]{:S(2)}) async-start(bf16[2,128,768]{2,1,0:T(8,128)(2,1)} %param.14), calls=%async_computation | async-start | bytes 786432 | tf_op jit(solution)/shard_map/all_to_all | solution.py:93
  44.2 18.2 %all-to-all-start.1 = ((f32[16,1,4608]{2,1,0:T(1,128)}), f32[16,1,4608]{2,1,0:T(1,128)S(1)}, u32[]{:S(2)}, u32[]{:S(2)}) async-start(f32[16,1,4608]{2,1,0:T(1,128)} %copy.104), calls=%async_computation.1 | async-start | bytes 589824 | tf_op jit(solution)/shard_map/all_to_all | solution.py:103
  62.4 10.7 %all-to-all-start.3 = ((bf16[2,128,768]{2,1,0:T(8,128)(2,1)}), bf16[2,128,768]{2,1,0:T(8,128)(2,1)S(1)}, u32[]{:S(2)}, u32[]{:S(2)}) async-start(bf16[2,128,768]{2,1,0:T(8,128)(2,1)} %param.16), calls=%async_computation.3 | async-start | bytes 786432 | tf_op jit(solution)/shard_map/all_to_all | solution.py:94
  66.4 332.0 %reduce-scatter.4.cloned.1.call-start = ((), (), s32[]{:S(2)}) async-start(), calls=%async_computation.11 | async-start | bytes 14800896
  73.4 46.5 %copy-start.6 = (bf16[256,768]{1,0:T(8,128)(2,1)}, bf16[256,768]{1,0:T(8,128)(2,1)S(1)}, u32[]{:S(2)}) copy-start(bf16[256,768]{1,0:T(8,128)(2,1)S(1)} %fusion.33) | copy-start | bytes 1179652
  180.6 3.2 copy-start.3
  183.5 10.3 %slice-start.2 = ((s8[5898240]{0:T(1024)(128)(4,1)}), s8[4194304]{0:T(1024)(128)(4,1)S(1)}, s32[]{:S(2)}) async-start(s8[5898240]{0:T(1024)(128)(4,1)} %bitcast.184), calls=%async_computation.14 | async-start | bytes 8388608
  183.8 5.6 %copy-start.7 = (bf16[256,768]{1,0:T(8,128)(2,1)S(1)}, bf16[256,768]{1,0:T(8,128)(2,1)}, u32[]{:S(2)}) copy-start(bf16[256,768]{1,0:T(8,128)(2,1)} %copy-done.6) | copy-start | bytes 1179652
  183.8 10.1 %slice-start.3 = ((s8[5898240]{0:T(1024)(128)(4,1)}), s8[1703936]{0:T(1024)(128)(4,1)S(1)}, s32[]{:S(2)}) async-start(s8[5898240]{0:T(1024)(128)(4,1)} %bitcast.184), calls=%async_computation.15 | async-start | bytes 3407872
  183.8 11.5 %slice-start = ((s8[4718592]{0:T(1024)(128)(4,1)}), s8[4194304]{0:T(1024)(128)(4,1)S(1)}, s32[]{:S(2)}) async-start(s8[4718592]{0:T(1024)(128)(4,1)} %bitcast.164), calls=%async_computation.12 | async-start | bytes 8388608
  189.3 4.5 %copy-start.17 = (bf16[256,3072]{1,0:T(8,128)(2,1)}, bf16[256,3072]{1,0:T(8,128)(2,1)S(1)}, u32[]{:S(2)}) copy-start(bf16[256,3072]{1,0:T(8,128)(2,1)S(1)} %get-tuple-element.31) | copy-start | bytes 4718596
  189.4 5.9 %slice-start.1 = ((s8[4718592]{0:T(1024)(128)(4,1)}), s8[524288]{0:T(1024)(128)(4,1)S(1)}, s32[]{:S(2)}) async-start(s8[4718592]{0:T(1024)(128)(4,1)} %bitcast.164), calls=%async_computation.13 | async-start | bytes 1048576
  199.5 0.8 copy-start.11
  207.5 1.9 copy-start.1
  220.0 3.2 copy-start.8
  220.0 3.2 copy-start.9
  220.0 3.2 copy-start.13
  224.2 5.0 %copy-start.18 = (bf16[256,3072]{1,0:T(8,128)(2,1)S(1)}, bf16[256,3072]{1,0:T(8,128)(2,1)}, u32[]{:S(2)}) copy-start(bf16[256,3072]{1,0:T(8,128)(2,1)} %copy-done.17) | copy-start | bytes 4718596
  229.2 3.8 copy-start.14
  233.0 3.0 copy-start.10
  233.0 3.0 copy-start.12
  238.2 1.0 copy-start.15
  244.2 10.8 %all-to-all-start.2 = ((bf16[2,2,49152]{2,1,0:T(2,128)(2,1)}), bf16[2,2,49152]{2,1,0:T(2,128)(2,1)S(1)}, u32[]{:S(2)}, u32[]{:S(2)}) async-start(bf16[2,2,49152]{2,1,0:T(2,128)(2,1)} %reshape.781), calls=%async_computation.2 | async-start | bytes 786432 | tf_op jit(solution)/shard_map/all_to_all | solution.py:149
  247.9 3.9 copy-start.4
  247.9 3.9 copy-start.5
  254.9 14.2 %all-to-all-start.4 = ((f32[1,256,768]{2,0,1:T(1,128)}), f32[1,256,768]{2,0,1:T(1,128)S(1)}, u32[]{:S(2)}, u32[]{:S(2)}) async-start(f32[1,256,768]{2,0,1:T(1,128)} %copy.113), calls=%async_computation.4 | async-start | bytes 1572864 | tf_op jit(solution)/shard_map/all_to_all | solution.py:197
  270.2 23.9 %all-to-all-start.5 = ((f32[32,1,4608]{2,1,0:T(1,128)}), f32[32,1,4608]{2,1,0:T(1,128)S(1)}, u32[]{:S(2)}, u32[]{:S(2)}) async-start(f32[32,1,4608]{2,1,0:T(1,128)} %broadcast_in_dim.11), calls=%async_computation.5 | async-start | bytes 1179648 | tf_op jit(solution)/shard_map/all_to_all | solution.py:209
  273.3 34.3 %copy-start.16 = (bf16[2,768]{1,0:T(2,128)(2,1)S(1)}, bf16[2,768]{1,0:T(2,128)(2,1)}, u32[]{:S(2)}) copy-start(bf16[2,768]{1,0:T(2,128)(2,1)} %param.15) | copy-start | bytes 9220
  295.1 11.1 %all-to-all-start.6 = ((f32[16,1,96]{2,1,0:T(1,128)}), f32[16,1,96]{2,1,0:T(1,128)S(1)}, u32[]{:S(2)}, u32[]{:S(2)}) async-start(f32[16,1,96]{2,1,0:T(1,128)} %bitcast.29), calls=%async_computation.6 | async-start | bytes 16384 | tf_op jit(solution)/shard_map/all_to_all | solution.py:263
  398.3 5.0 %copy-start.2 = (bf16[24,9344]{1,0:T(8,128)(2,1)S(1)}, bf16[24,9344]{1,0:T(8,128)(2,1)}, u32[]{:S(2)}) copy-start(bf16[24,9344]{1,0:T(8,128)(2,1)} %reduce-scatter.4.cloned.1.call-done) | copy-start | bytes 1345540
Sparse Core Ops, SparseCore 0:
  10.3 55.5 all-gather.3
  68.2 51.5 all-gather.7
  122.7 57.8 all-gather.5
  238.3 159.9 reduce-scatter.3
